TPU v7x, 32 devices: a whole 2x2x4 slice. The times are simulated.
32 devices in a mesh: row: 8 (over z, x), col: 4 (over y, core).
Axes of the slice: x: 2, y: 2, z: 4, core: 2. Of those that a mesh axis runs over, the one named last changes fastest.
Arguments:
- start_block: float32 [8, 32768], P(None, ('row', 'col')), may hold values from -6 to 6
- blocks: bfloat16 [8, 4, 128, 128, 128], P('row', 'col'), as said below
- block_rows: int32 [8, 4, 128], P(None, 'col'), may hold values from 0 to 31, as said below
- block_cols: int32 [8, 4, 128], P(None, 'col'), may hold values from 0 to 63, as said below
- counts: int32 [8, 4], replicated, may hold values from 1 to 128, as said below
Outputs:
- next_block: float32 [8, 32768], P(None, ('row', 'col'))
- tridiagonal: float32 [16, 16], replicated
Inputs may be any that keep to these rules, and one draw needn't show every extreme that they name: `block_rows`: entries of each tile are local block rows below 32; within a tile the used slots name distinct blocks whose global row block is at or after the global column block; slots at or after counts are 0 and not part of H. `block_cols`: local block columns below 64, paired with block_rows; unused slots are 0. `counts`: some tile holds exactly 128 blocks in every draw. Blocks whose global row and column blocks agree are symmetric.
All inputs are finite; a program needn't handle non-finite values.
Results may differ from a plain program's by a relative error of at most 0.0048.
Values may be sent and summed in bfloat16 or wider, within the bound.
No kernel may reach another device: no remote copies, remote signals or barrier semaphores. Data moves between devices by JAX's collectives and lax.ppermute only.
A program may use at most 64 MiB of HBM per device.

v0:
```python
import math
import jax
import jax.numpy as jnp
from jax import lax
from jax.sharding import PartitionSpec as P

ITERS = 2
blocks_per_step = 16


def accumulate(
    stored,
    row_list,
    col_list,
    first_slot,
    live_count,
    tile_row,
    tile_col,
    shape_info,
    row_vector,
    col_vector,
    totals,
):
    row_blocks, col_blocks, piece_blocks, grid_cols = shape_info
    vectors = row_vector.shape[0]
    block_side = stored.shape[-1]
    slot_total = stored.shape[0]
    row_pieces = row_vector.reshape(vectors, row_blocks, block_side)
    col_pieces = col_vector.reshape(vectors, col_blocks, block_side)
    offsets = jnp.arange(blocks_per_step, dtype=jnp.int32)
    row_range = jnp.arange(row_blocks, dtype=jnp.int32)
    col_range = jnp.arange(col_blocks, dtype=jnp.int32)

    def visit(group_index, running):
        row_total, col_total = running
        local_slot = group_index * blocks_per_step + offsets
        is_valid = local_slot < live_count
        slot_ids = jnp.clip(first_slot + local_slot, 0, slot_total - 1)
        tile_data = jnp.take(stored, slot_ids, axis=0)
        row_ids = jnp.take(row_list, slot_ids)
        col_ids = jnp.take(col_list, slot_ids)
        global_row = tile_row * row_blocks + row_ids
        global_col = (
            col_ids // piece_blocks * grid_cols + tile_col
        ) * piece_blocks + col_ids % piece_blocks
        mirror = is_valid & (global_row != global_col)
        col_taken = jnp.take(col_pieces, col_ids, axis=1)
        row_taken = jnp.take(row_pieces, row_ids, axis=1)
        direct = jnp.einsum(
            "gij,kgj->kgi", tile_data, col_taken, preferred_element_type=jnp.float32
        )
        turned = jnp.einsum(
            "gji,kgj->kgi", tile_data, row_taken, preferred_element_type=jnp.float32
        )
        pick_rows = ((row_ids[:, None] == row_range[None, :]) & is_valid[:, None]).astype(
            jnp.float32
        )
        pick_cols = ((col_ids[:, None] == col_range[None, :]) & mirror[:, None]).astype(jnp.float32)
        row_total = row_total + jnp.einsum(
            "gs,kgi->ksi", pick_rows, direct, precision=lax.Precision.HIGHEST
        )
        col_total = col_total + jnp.einsum(
            "gs,kgi->ksi", pick_cols, turned, precision=lax.Precision.HIGHEST
        )
        return (row_total, col_total)

    group_count = (live_count + blocks_per_step - 1) // blocks_per_step
    return lax.fori_loop(0, group_count, visit, totals)


def per_device(start_block, blocks, block_rows, block_cols, counts):
    highest = lax.Precision.HIGHEST
    vectors, piece_len = start_block.shape
    stored = blocks[0, 0]
    block_side = stored.shape[-1]
    grid_rows = lax.axis_size("row")
    grid_cols = lax.axis_size("col")
    piece_blocks = piece_len // block_side
    row_blocks = grid_cols * piece_blocks
    col_blocks = grid_rows * piece_blocks
    shape_info = (row_blocks, col_blocks, piece_blocks, grid_cols)
    tile_row = lax.axis_index("row")
    tile_col = lax.axis_index("col")
    row_lists = block_rows[:, 0, :]
    col_lists = block_cols[:, 0, :]
    own_count = counts[tile_row, tile_col]
    own_rows = row_lists[tile_row]
    own_cols = col_lists[tile_row]
    start_sum = lax.psum(jnp.dot(start_block, start_block.T, precision=highest), ("row", "col"))
    factor = jnp.linalg.cholesky(start_sum)
    current = lax.linalg.triangular_solve(factor, start_block, left_side=True, lower=True)
    previous = current
    prev_factor = factor
    diagonals = []
    couplings = []
    for step_index in range(ITERS):
        half_block = current.astype(jnp.bfloat16)
        row_vector = lax.all_gather(half_block, "col", axis=1, tiled=True)
        col_vector = lax.all_gather(half_block, "row", axis=1, tiled=True)
        row_zero = jnp.zeros((vectors, row_blocks, block_side), jnp.float32)
        col_zero = jnp.zeros((vectors, col_blocks, block_side), jnp.float32)
        row_total, col_total = accumulate(
            stored,
            own_rows,
            own_cols,
            0,
            own_count,
            tile_row,
            tile_col,
            shape_info,
            row_vector,
            col_vector,
            (row_zero, col_zero),
        )
        row_part = lax.psum_scatter(
            row_total.reshape(vectors, row_blocks * block_side),
            "col",
            scatter_dimension=1,
            tiled=True,
        )
        col_part = lax.psum_scatter(
            col_total.reshape(vectors, col_blocks * block_side),
            "row",
            scatter_dimension=1,
            tiled=True,
        )
        image = row_part + col_part
        if step_index > 0:
            image = image - jnp.dot(prev_factor.T, previous, precision=highest)
        local_proj = jnp.dot(current, image.T, precision=highest)
        local_square = jnp.dot(image, image.T, precision=highest)
        projection, squares = lax.psum((local_proj, local_square), ("row", "col"))
        image = image - jnp.dot(projection.T, current, precision=highest)
        gram = squares - jnp.dot(projection.T, projection, precision=highest)
        factor = jnp.linalg.cholesky(gram)
        following = lax.linalg.triangular_solve(factor, image, left_side=True, lower=True)
        diagonals.append(projection)
        couplings.append(factor)
        previous, prev_factor, current = (current, factor, following)
    tri_size = ITERS * vectors
    tridiagonal = jnp.zeros((tri_size, tri_size), jnp.float32)
    for step_index in range(ITERS):
        low = step_index * vectors
        tridiagonal = tridiagonal.at[low : low + vectors, low : low + vectors].set(
            diagonals[step_index]
        )
        if step_index + 1 < ITERS:
            tridiagonal = tridiagonal.at[
                low : low + vectors, low + vectors : low + 2 * vectors
            ].set(couplings[step_index])
            tridiagonal = tridiagonal.at[
                low + vectors : low + 2 * vectors, low : low + vectors
            ].set(couplings[step_index].T)
    order_root = math.sqrt(piece_len * grid_rows * grid_cols)
    return (current * order_root, tridiagonal)


def solution(mesh):
    placed = (
        P(None, ("row", "col")),
        P("row", "col", None, None, None),
        P(None, "col", None),
        P(None, "col", None),
        P(),
    )
    return jax.shard_map(
        per_device,
        mesh=mesh,
        in_specs=placed,
        out_specs=(P(None, ("row", "col")), P()),
        check_vma=False,
    )
```

profile of v0, /device:TPU:0, one launch (start us, length us, event | category | flops | bytes accessed | tf_op | source)
XLA Modules:
  0.0 520.5 jit_solution(15743571645493684998)
XLA Ops:
  7.2 1.3 dynamic_slice.9
  9.4 41.9 %psum.35 = f32[8,8]{0,1:T(8,128)S(1)} all-reduce(f32[8,8]{0,1:T(8,128)S(1)} %fusion.100), channel_id=1, replica_groups=mesh['row'=8,'col'=4] {'row','col'}, use_global_device_ids=true, to_apply=%region_0.0 | all-reduce | flops 64 | bytes 512 | tf_op jit(solution)/shard_map/psum | solution.py:89
  51.5 0.7 cholesky.59
  54.4 5.5 %all_gather.13 = bf16[8,4096]{1,0:T(8,128)(2,1)S(1)} all-gather(bf16[8,1024]{1,0:T(8,128)(2,1)S(1)} %get-tuple-element.597), channel_id=1, replica_groups=mesh['row'=8,'col'=4] {'col'}, dimensions={1}, use_global_device_ids=true | all-gather | bytes 81920 | tf_op jit(solution)/shard_map/all_gather | solution.py:98
  59.9 30.5 %all_gather.12 = bf16[8,8192]{1,0:T(8,128)(2,1)S(1)} all-gather(bf16[8,1024]{1,0:T(8,128)(2,1)S(1)} %get-tuple-element.597), channel_id=1, replica_groups=mesh['row'=8,'col'=4] {'row'}, dimensions={1}, use_global_device_ids=true | all-gather | bytes 147456 | tf_op jit(solution)/shard_map/all_gather | solution.py:99
  90.4 0.7 dynamic-slice_bitcast_fusion
  91.1 7.7 %while.34 = (s32[]{:T(128)}, f32[8,32,128]{2,1,0:T(8,128)S(1)}, f32[8,64,128]{2,1,0:T(8,128)S(1)}, s32[]{:T(128)}, s32[128]{0:T(128)S(1)}, /*index=5*/bf16[8,64,...) while((s32[]{:T(128)}, f32[8,32,128]{2,1,0:T(8,128)S(1)}, ...), condition=%wide.region_4.11_spmd.clone, body=%wide.region_3.10_spmd.clone.sunk | while | flops 27925444 | bytes 3356565 | solution.py:68
  92.5 0.7 compare_and_fusion.14
  94.4 2.8 gather_fusion
  98.8 0.7 copy.71
  99.6 0.8 copy.69
  100.6 0.7 and_reduce_fusion
  101.9 71.0 %reduce-scatter.5.cloned.1.call-done = f32[8,1024]{1,0:T(8,128)} async-done(((f32[8,4096]{1,0:T(8,128)}), f32[8,1024]{1,0:T(8,128)}) %reduce-scatter.5.cloned.1.call-update) | async-done | bytes 32784 | tf_op jit(solution)/shard_map/reduce_scatter | solution.py:115
  172.9 65.4 %reduce-scatter.7.cloned.1.call-done = f32[8,1024]{1,0:T(8,128)} async-done(((f32[8,8192]{1,0:T(8,128)}), f32[8,1024]{1,0:T(8,128)}) %reduce-scatter.7.cloned.1.call-update) | async-done | bytes 32784 | tf_op jit(solution)/shard_map/reduce_scatter | solution.py:121
  238.3 0.8 add.228
  239.4 40.2 %all-reduce.2 = (f32[8,8]{1,0:T(8,128)S(1)}, f32[8,8]{0,1:T(8,128)S(1)}) all-reduce(f32[8,8]{1,0:T(8,128)S(1)} %fusion.102, f32[8,8]{0,1:T(8,128)S(1)} %fusion.101), channel_id=1, replica_groups=mesh['row'=8,'col'=4] {'row','col'}, use_global_device_ids=true, to_apply=%region_8.15 | all-reduce | flops 128 | bytes 1024 | tf_op jit(solution)/shard_map/psum | solution.py:132
  280.1 0.7 cholesky.70
  281.5 2.6 fusion.91
  285.0 5.5 %all_gather.15 = bf16[8,4096]{1,0:T(8,128)(2,1)S(1)} all-gather(bf16[8,1024]{1,0:T(8,128)(2,1)S(1)} %get-tuple-element.599), channel_id=1, replica_groups=mesh['row'=8,'col'=4] {'col'}, dimensions={1}, use_global_device_ids=true | all-gather | bytes 81920 | tf_op jit(solution)/shard_map/all_gather | solution.py:98
  290.5 30.5 %all_gather.14 = bf16[8,8192]{1,0:T(8,128)(2,1)S(1)} all-gather(bf16[8,1024]{1,0:T(8,128)(2,1)S(1)} %get-tuple-element.599), channel_id=1, replica_groups=mesh['row'=8,'col'=4] {'row'}, dimensions={1}, use_global_device_ids=true | all-gather | bytes 147456 | tf_op jit(solution)/shard_map/all_gather | solution.py:99
  321.1 7.7 %while.35 = (s32[]{:T(128)}, f32[8,32,128]{2,1,0:T(8,128)S(1)}, f32[8,64,128]{2,1,0:T(8,128)S(1)}, s32[]{:T(128)}, s32[128]{0:T(128)S(1)}, /*index=5*/bf16[8,64,...) while((s32[]{:T(128)}, f32[8,32,128]{2,1,0:T(8,128)S(1)}, ...), condition=%wide.region_10.17_spmd.clone, body=%wide.region_9.16_spmd.clone.sunk | while | flops 27925444 | bytes 3356565 | solution.py:68
  322.4 0.7 compare_and_fusion.17
  324.4 2.8 gather_fusion.5
  328.8 0.7 copy.70
  329.6 0.9 copy.68
  330.6 1.8 scatter.15
  332.8 69.3 %reduce-scatter.9.cloned.1.call-done = f32[8,1024]{1,0:T(8,128)} async-done(((f32[8,4096]{1,0:T(8,128)}), f32[8,1024]{1,0:T(8,128)}) %reduce-scatter.9.cloned.1.call-update) | async-done | bytes 32784 | tf_op jit(solution)/shard_map/reduce_scatter | solution.py:115
  402.1 65.3 %reduce-scatter.11.cloned.1.call-done = f32[8,1024]{1,0:T(8,128)} async-done(((f32[8,8192]{1,0:T(8,128)}), f32[8,1024]{1,0:T(8,128)}) %reduce-scatter.11.cloned.1.call-update) | async-done | bytes 32784 | tf_op jit(solution)/shard_map/reduce_scatter | solution.py:121
  467.4 1.6 convolution_subtract_fusion.1
  469.3 40.2 %all-reduce.1 = (f32[8,8]{1,0:T(8,128)S(1)}, f32[8,8]{0,1:T(8,128)S(1)}) all-reduce(f32[8,8]{1,0:T(8,128)S(1)} %fusion.104, f32[8,8]{0,1:T(8,128)S(1)} %fusion.103), channel_id=1, replica_groups=mesh['row'=8,'col'=4] {'row','col'}, use_global_device_ids=true, to_apply=%region_14.21 | all-reduce | flops 128 | bytes 1024 | tf_op jit(solution)/shard_map/psum | solution.py:132
  510.4 0.7 cholesky.81
  513.1 0.9 convolution_multiply_fusion
  (82 shorter events, 17.6 us)
Async XLA Ops:
  7.2 2.1 copy-start
  7.2 165.7 %reduce-scatter.5.cloned.1.call-start = ((), (), s32[]{:S(2)}) async-start(), calls=%async_computation.4 | async-start | bytes 163840 | tf_op jit(solution)/shard_map/reduce_scatter | solution.py:115
  99.6 138.7 %reduce-scatter.7.cloned.1.call-start = ((), (), s32[]{:S(2)}) async-start(), calls=%async_computation.5 | async-start | bytes 294912 | tf_op jit(solution)/shard_map/reduce_scatter | solution.py:121
  100.5 301.6 %reduce-scatter.9.cloned.1.call-start = ((), (), s32[]{:S(2)}) async-start(), calls=%async_computation.6 | async-start | bytes 163840 | tf_op jit(solution)/shard_map/reduce_scatter | solution.py:115
  329.6 137.8 %reduce-scatter.11.cloned.1.call-start = ((), (), s32[]{:S(2)}) async-start(), calls=%async_computation.7 | async-start | bytes 294912 | tf_op jit(solution)/shard_map/reduce_scatter | solution.py:121
  510.4 3.6 copy-start.1
Sparse Core Ops, SparseCore 0:
  99.7 73.1 reduce-scatter.4
  176.2 62.0 reduce-scatter.6
  329.7 72.3 reduce-scatter.8
  405.3 62.0 reduce-scatter.10
where the time goes:
time: 522 us; the launch traced here: 521 us
  waiting for transfers between devices  271 us (52%)
  blocking collectives  194 us (37%)
  local copies, waits for them, and re-layouts  19.4 us (4%)
  between operations  14.6 us (3%)
  other arithmetic  13.1 us (3%)
  matrix products  7.66 us (1%)
    reduce_scatter x2, waiting for transfers between devices, per_device(): lax.psum_scatter(row_total.reshape(vectors, row_blocks * block_side), 'co...  140 us
    reduce_scatter x2, waiting for transfers between devices, per_device(): lax.psum_scatter(col_total.reshape(vectors, col_blocks * block_side), 'ro...  131 us
    psum x2, blocking collectives, per_device(): projection, squares = lax.psum((local_proj, local_square), ('row', 'col'))  80.4 us
    all_gather x2, blocking collectives, per_device(): col_vector = lax.all_gather(half_block, 'row', axis=1, tiled=True)  61 us
    psum x1, blocking collectives, per_device(): lax.psum(jnp.dot(start_block, start_block.T, precision=highest), ('row',...  41.9 us
    all_gather x2, blocking collectives, per_device(): row_vector = lax.all_gather(half_block, 'col', axis=1, tiled=True)  11 us
  transfers between devices with their start and end apart: 4, of which 4 were waited for; matrix products, arithmetic and copies ran while one was open for 1% of the time, Pallas kernels for 0%

commit v1 on v0

--- a/solution.py
+++ b/solution.py
@@ -6,6 +6,10 @@
 
 ITERS = 2
 blocks_per_step = 16
+
+
+def note_regions(field_in):
+    return jax.lax.psum(jax.lax.psum(field_in, axis_name="row"), "col")
 
 
 def accumulate(
@@ -86,7 +90,7 @@
     own_count = counts[tile_row, tile_col]
     own_rows = row_lists[tile_row]
     own_cols = col_lists[tile_row]
-    start_sum = lax.psum(jnp.dot(start_block, start_block.T, precision=highest), ("row", "col"))
+    start_sum = note_regions(jnp.dot(start_block, start_block.T, precision=highest))
     factor = jnp.linalg.cholesky(start_sum)
     current = lax.linalg.triangular_solve(factor, start_block, left_side=True, lower=True)
     previous = current

time: 522 us -> 506 us (0.969)
  blocking collectives: 194 us -> 181 us
    psum x1 -> x2, blocking collectives: 41.9 us -> 28.8 us  [note_regions(): return jax.lax.psum(jax.lax.psum(field_in, axis_name='row'), 'col')]
where the time goes in v1:
time: 506 us; the launch traced here: 504 us
  waiting for transfers between devices  269 us (53%)
  blocking collectives  181 us (36%)
  local copies, waits for them, and re-layouts  19.4 us (4%)
  between operations  14.6 us (3%)
  other arithmetic  13.1 us (3%)
  matrix products  7.65 us (2%)
    reduce_scatter x2, waiting for transfers between devices, per_device(): lax.psum_scatter(row_total.reshape(vectors, row_blocks * block_side), 'co...  138 us
    reduce_scatter x2, waiting for transfers between devices, per_device(): lax.psum_scatter(col_total.reshape(vectors, col_blocks * block_side), 'ro...  131 us
    psum x2, blocking collectives, per_device(): projection, squares = lax.psum((local_proj, local_square), ('row', 'col'))  80.3 us
    all_gather x2, blocking collectives, per_device(): col_vector = lax.all_gather(half_block, 'row', axis=1, tiled=True)  61 us
    psum x2, blocking collectives, note_regions(): return jax.lax.psum(jax.lax.psum(field_in, axis_name='row'), 'col')  28.8 us
    all_gather x2, blocking collectives, per_device(): row_vector = lax.all_gather(half_block, 'col', axis=1, tiled=True)  10.7 us
  transfers between devices with their start and end apart: 4, of which 4 were waited for; matrix products, arithmetic and copies ran while one was open for 1% of the time, Pallas kernels for 0%

profile of v1, /device:TPU:0, one launch (start us, length us, event | category | flops | bytes accessed | tf_op | source)
XLA Modules:
  0.0 504.5 jit_solution(1432146174159704399)
XLA Ops:
  7.2 1.3 dynamic_slice.9
  9.4 23.1 %psum.42 = f32[8,8]{0,1:T(8,128)S(1)} all-reduce(f32[8,8]{0,1:T(8,128)S(1)} %fusion.100), channel_id=1, replica_groups=mesh['row'=8,'col'=4] {'row'}, use_global_device_ids=true, to_apply=%region_0.0 | all-reduce | flops 64 | bytes 512 | tf_op jit(solution)/shard_map/psum | solution.py:12
  32.6 5.7 %psum.43 = f32[8,8]{0,1:T(8,128)S(1)} all-reduce(f32[8,8]{0,1:T(8,128)S(1)} %psum.42), channel_id=1, replica_groups=mesh['row'=8,'col'=4] {'col'}, use_global_device_ids=true, to_apply=%region_1.0 | all-reduce | flops 64 | bytes 512 | tf_op jit(solution)/shard_map/psum | solution.py:12
  38.3 0.7 cholesky.59
  41.2 5.2 %all_gather.13 = bf16[8,4096]{1,0:T(8,128)(2,1)S(1)} all-gather(bf16[8,1024]{1,0:T(8,128)(2,1)S(1)} %get-tuple-element.597), channel_id=1, replica_groups=mesh['row'=8,'col'=4] {'col'}, dimensions={1}, use_global_device_ids=true | all-gather | bytes 81920 | tf_op jit(solution)/shard_map/all_gather | solution.py:102
  46.5 30.5 %all_gather.12 = bf16[8,8192]{1,0:T(8,128)(2,1)S(1)} all-gather(bf16[8,1024]{1,0:T(8,128)(2,1)S(1)} %get-tuple-element.597), channel_id=1, replica_groups=mesh['row'=8,'col'=4] {'row'}, dimensions={1}, use_global_device_ids=true | all-gather | bytes 147456 | tf_op jit(solution)/shard_map/all_gather | solution.py:103
  77.7 7.7 %while.34 = (s32[]{:T(128)}, f32[8,32,128]{2,1,0:T(8,128)S(1)}, f32[8,64,128]{2,1,0:T(8,128)S(1)}, s32[]{:T(128)}, s32[128]{0:T(128)S(1)}, /*index=5*/bf16[8,64,...) while((s32[]{:T(128)}, f32[8,32,128]{2,1,0:T(8,128)S(1)}, ...), condition=%wide.region_5.12_spmd.clone, body=%wide.region_4.11_spmd.clone.sunk | while | flops 27925444 | bytes 3356565 | solution.py:72
  79.1 0.7 compare_and_fusion.14
  81.0 2.8 gather_fusion
  85.4 0.7 copy.71
  86.2 0.8 copy.69
  87.2 0.7 and_reduce_fusion
  88.5 68.4 %reduce-scatter.5.cloned.1.call-done = f32[8,1024]{1,0:T(8,128)} async-done(((f32[8,4096]{1,0:T(8,128)}), f32[8,1024]{1,0:T(8,128)}) %reduce-scatter.5.cloned.1.call-update) | async-done | bytes 32784 | tf_op jit(solution)/shard_map/reduce_scatter | solution.py:119
  157.0 65.4 %reduce-scatter.7.cloned.1.call-done = f32[8,1024]{1,0:T(8,128)} async-done(((f32[8,8192]{1,0:T(8,128)}), f32[8,1024]{1,0:T(8,128)}) %reduce-scatter.7.cloned.1.call-update) | async-done | bytes 32784 | tf_op jit(solution)/shard_map/reduce_scatter | solution.py:125
  222.4 0.8 add.230
  223.5 40.1 %all-reduce.2 = (f32[8,8]{1,0:T(8,128)S(1)}, f32[8,8]{0,1:T(8,128)S(1)}) all-reduce(f32[8,8]{1,0:T(8,128)S(1)} %fusion.102, f32[8,8]{0,1:T(8,128)S(1)} %fusion.101), channel_id=1, replica_groups=mesh['row'=8,'col'=4] {'row','col'}, use_global_device_ids=true, to_apply=%region_9.16 | all-reduce | flops 128 | bytes 1024 | tf_op jit(solution)/shard_map/psum | solution.py:136
  264.1 0.7 cholesky.70
  265.6 2.6 fusion.91
  269.0 5.5 %all_gather.15 = bf16[8,4096]{1,0:T(8,128)(2,1)S(1)} all-gather(bf16[8,1024]{1,0:T(8,128)(2,1)S(1)} %get-tuple-element.599), channel_id=1, replica_groups=mesh['row'=8,'col'=4] {'col'}, dimensions={1}, use_global_device_ids=true | all-gather | bytes 81920 | tf_op jit(solution)/shard_map/all_gather | solution.py:102
  274.5 30.5 %all_gather.14 = bf16[8,8192]{1,0:T(8,128)(2,1)S(1)} all-gather(bf16[8,1024]{1,0:T(8,128)(2,1)S(1)} %get-tuple-element.599), channel_id=1, replica_groups=mesh['row'=8,'col'=4] {'row'}, dimensions={1}, use_global_device_ids=true | all-gather | bytes 147456 | tf_op jit(solution)/shard_map/all_gather | solution.py:103
  305.1 7.7 %while.35 = (s32[]{:T(128)}, f32[8,32,128]{2,1,0:T(8,128)S(1)}, f32[8,64,128]{2,1,0:T(8,128)S(1)}, s32[]{:T(128)}, s32[128]{0:T(128)S(1)}, /*index=5*/bf16[8,64,...) while((s32[]{:T(128)}, f32[8,32,128]{2,1,0:T(8,128)S(1)}, ...), condition=%wide.region_11.18_spmd.clone, body=%wide.region_10.17_spmd.clone.sunk | while | flops 27925444 | bytes 3356565 | solution.py:72
  306.5 0.7 compare_and_fusion.17
  308.4 2.8 gather_fusion.5
  312.8 0.7 copy.70
  313.6 0.9 copy.68
  314.6 1.8 scatter.15
  316.8 69.3 %reduce-scatter.9.cloned.1.call-done = f32[8,1024]{1,0:T(8,128)} async-done(((f32[8,4096]{1,0:T(8,128)}), f32[8,1024]{1,0:T(8,128)}) %reduce-scatter.9.cloned.1.call-update) | async-done | bytes 32784 | tf_op jit(solution)/shard_map/reduce_scatter | solution.py:119
  386.1 65.2 %reduce-scatter.11.cloned.1.call-done = f32[8,1024]{1,0:T(8,128)} async-done(((f32[8,8192]{1,0:T(8,128)}), f32[8,1024]{1,0:T(8,128)}) %reduce-scatter.11.cloned.1.call-update) | async-done | bytes 32784 | tf_op jit(solution)/shard_map/reduce_scatter | solution.py:125
  451.4 1.6 convolution_subtract_fusion.1
  453.3 40.1 %all-reduce.1 = (f32[8,8]{1,0:T(8,128)S(1)}, f32[8,8]{0,1:T(8,128)S(1)}) all-reduce(f32[8,8]{1,0:T(8,128)S(1)} %fusion.104, f32[8,8]{0,1:T(8,128)S(1)} %fusion.103), channel_id=1, replica_groups=mesh['row'=8,'col'=4] {'row','col'}, use_global_device_ids=true, to_apply=%region_15.22 | all-reduce | flops 128 | bytes 1024 | tf_op jit(solution)/shard_map/psum | solution.py:136
  494.4 0.7 cholesky.81
  497.1 0.9 convolution_multiply_fusion
  (83 shorter events, 18.3 us)
Async XLA Ops:
  7.2 2.1 copy-start
  7.2 149.8 %reduce-scatter.5.cloned.1.call-start = ((), (), s32[]{:S(2)}) async-start(), calls=%async_computation.4 | async-start | bytes 163840 | tf_op jit(solution)/shard_map/reduce_scatter | solution.py:119
  86.2 136.2 %reduce-scatter.7.cloned.1.call-start = ((), (), s32[]{:S(2)}) async-start(), calls=%async_computation.5 | async-start | bytes 294912 | tf_op jit(solution)/shard_map/reduce_scatter | solution.py:125
  87.1 299.0 %reduce-scatter.9.cloned.1.call-start = ((), (), s32[]{:S(2)}) async-start(), calls=%async_computation.6 | async-start | bytes 163840 | tf_op jit(solution)/shard_map/reduce_scatter | solution.py:119
  313.6 137.8 %reduce-scatter.11.cloned.1.call-start = ((), (), s32[]{:S(2)}) async-start(), calls=%async_computation.7 | async-start | bytes 294912 | tf_op jit(solution)/shard_map/reduce_scatter | solution.py:125
  494.3 3.6 copy-start.1
Sparse Core Ops, SparseCore 0:
  86.3 70.6 reduce-scatter.4
  160.3 62.0 reduce-scatter.6
  313.7 72.3 reduce-scatter.8
  389.3 62.0 reduce-scatter.10
